TPU v7x, 32 devices: a whole 2x2x4 slice. The times are simulated.
32 devices in a mesh: seq: 16 (over z, y, x), dp: 2 (over core).
Axes of the slice: x: 2, y: 2, z: 4, core: 2. Of those that a mesh axis runs over, the one named last changes fastest.
Arguments:
- glu_input: bfloat16 [2, 12288, 1024], P('dp', 'seq'), may hold values from -2500 to 2500
- out_grad: bfloat16 [2, 12288, 1024], P('dp', 'seq'), may hold values from -50 to 50
- lengths: int32 [2], replicated, may hold values from 6144 to 12288, as said below
- depth_weight: float32 [512, 31], replicated, may hold values from -1.5 to 1.5
- bn_gain: float32 [512], replicated, may hold values from 0.5 to 2
- bn_shift: float32 [512], replicated, may hold values from -1 to 1
- proj_weight: bfloat16 [512, 1024], P('seq', 'dp'), may hold values from -0.25 to 0.25
Outputs:
- input_grad: bfloat16 [2, 12288, 1024], P('dp', 'seq')
- proj_grad: float32 [512, 1024], P('seq', 'dp')
- depth_grad: float32 [512, 31], P('seq')
- gain_grad: float32 [512], P('seq')
- shift_grad: float32 [512], P('seq')
Inputs may be any that keep to these rules, and one draw needn't show every extreme that they name: `lengths`: at least one utterance has all 12288 frames valid.
All inputs are finite; a program needn't handle non-finite values.
Results may differ from a plain program's by a relative error of at most 0.0061.
Values may be sent and summed in bfloat16 or wider, within the bound.
A program may use at most 64 MiB of HBM per device.

v0:
```python
import jax
import jax.numpy as jnp
from jax import lax
from jax.sharding import PartitionSpec as P

EPSILON = 1e-05


def with_halo(block, sides, width):
    for axis, dim in sides:
        count = lax.axis_size(axis)
        forward = [(i, i + 1) for i in range(count - 1)]
        backward = [(target, source) for source, target in forward]
        low = lax.ppermute(
            lax.slice_in_dim(block, block.shape[dim] - width, None, axis=dim), axis, forward
        )
        high = lax.ppermute(lax.slice_in_dim(block, 0, width, axis=dim), axis, backward)
        block = jnp.concatenate([low, block, high], axis=dim)
    return block


def on_device(glu_input, out_grad, lengths, depth_weight, bn_gain, bn_shift, proj_weight):
    utt_dev, frames_dev, doubled = glu_input.shape
    channels = doubled // 2
    kernel = depth_weight.shape[1]
    half_width = (kernel - 1) // 2
    seq_count = lax.axis_size("seq")
    grad_scale = float(utt_dev * lax.axis_size("dp") * frames_dev * seq_count) ** (-0.5)
    positions = lax.axis_index("seq") * frames_dev + jnp.arange(frames_dev, dtype=jnp.int32)
    own_lengths = lax.dynamic_slice_in_dim(lengths, lax.axis_index("dp") * utt_dev, utt_dev)
    frame_mask = (positions[None, :] < own_lengths[:, None]).astype(jnp.float32)[:, :, None]
    frame_count = jnp.sum(lengths).astype(jnp.float32)
    values = glu_input[:, :, :channels].astype(jnp.float32)
    gate_sigmoid = jax.nn.sigmoid(glu_input[:, :, channels:].astype(jnp.float32))
    glu_out = (values * gate_sigmoid * frame_mask).astype(jnp.bfloat16)
    padded = with_halo(glu_out, (("seq", 1),), half_width).astype(jnp.float32)
    conv_out = jnp.zeros((utt_dev, frames_dev, channels), jnp.float32)
    for offset in range(kernel):
        conv_out = conv_out + depth_weight[:, offset] * padded[:, offset : offset + frames_dev]
    conv_total, squares = lax.psum(
        (
            jnp.sum(frame_mask * conv_out, axis=(0, 1)),
            jnp.sum(frame_mask * conv_out * conv_out, axis=(0, 1)),
        ),
        ("seq", "dp"),
    )
    mean_val = conv_total / frame_count
    variance = squares / frame_count - mean_val * mean_val
    inv_std = lax.rsqrt(variance + EPSILON)
    normed = (conv_out - mean_val) * inv_std
    pre_act = bn_gain * normed + bn_shift
    pre_sig = jax.nn.sigmoid(pre_act)
    act_out = (frame_mask * pre_act * pre_sig).astype(jnp.bfloat16)
    proj_rows = lax.all_gather(proj_weight, "dp", axis=1, tiled=True)
    act_grad = frame_mask * jnp.einsum(
        "btd,cd->btc",
        out_grad,
        lax.all_gather(proj_rows, "seq", axis=0, tiled=True),
        preferred_element_type=jnp.float32,
    )
    pre_grad = act_grad * pre_sig * (1.0 + pre_act * (1.0 - pre_sig))
    gain_sum, shift_sum = lax.psum(
        (jnp.sum(pre_grad * normed, axis=(0, 1)), jnp.sum(pre_grad, axis=(0, 1))), ("seq", "dp")
    )
    conv_grad = (
        frame_mask
        * inv_std
        * bn_gain
        * (pre_grad - shift_sum / frame_count - normed * gain_sum / frame_count)
    ).astype(jnp.bfloat16)
    conv_wide = conv_grad.astype(jnp.float32)
    weight_terms = (
        jnp.einsum("btc,btd->cd", act_out, out_grad, preferred_element_type=jnp.float32)
        * grad_scale
    )
    depth_terms = (
        jnp.stack(
            [
                jnp.sum(conv_wide * padded[:, offset : offset + frames_dev], axis=(0, 1))
                for offset in range(kernel)
            ],
            axis=1,
        )
        * grad_scale
    )
    beside_all = with_halo(conv_grad, (("seq", 1),), half_width).astype(jnp.float32)
    glu_grad = jnp.zeros((utt_dev, frames_dev, channels), jnp.float32)
    for offset in range(kernel):
        glu_grad = (
            glu_grad
            + depth_weight[:, offset]
            * beside_all[:, 2 * half_width - offset : 2 * half_width - offset + frames_dev]
        )
    glu_grad = glu_grad * frame_mask
    input_grad = jnp.concatenate(
        [glu_grad * gate_sigmoid, glu_grad * values * gate_sigmoid * (1.0 - gate_sigmoid)], axis=2
    ).astype(jnp.bfloat16)
    proj_part, depth_part = (
        lax.psum_scatter(weight_terms, "seq", scatter_dimension=0, tiled=True),
        lax.psum_scatter(depth_terms, "seq", scatter_dimension=0, tiled=True),
    )
    proj_grad = lax.psum_scatter(proj_part, "dp", scatter_dimension=1, tiled=True)
    depth_grad = lax.psum(depth_part, "dp")
    per_device = channels // seq_count
    first_channel = lax.axis_index("seq") * per_device
    gain_grad = lax.dynamic_slice_in_dim(gain_sum, first_channel, per_device) * grad_scale
    shift_grad = lax.dynamic_slice_in_dim(shift_sum, first_channel, per_device) * grad_scale
    return (input_grad, proj_grad, depth_grad, gain_grad, shift_grad)


def solution(mesh):
    return jax.shard_map(
        on_device,
        mesh=mesh,
        in_specs=(P("dp", "seq", None), P("dp", "seq", None), P(), P(), P(), P(), P("seq", "dp")),
        out_specs=(P("dp", "seq", None), P("seq", "dp"), P("seq", None), P("seq"), P("seq")),
        check_vma=False,
    )
```

profile of v0, /device:TPU:0, one launch (start us, length us, event | category | flops | bytes accessed | tf_op | source)
XLA Modules:
  0.0 252.0 jit_solution(1266124155400691946)
XLA Ops:
  7.2 3.7 %all_gather.6 = bf16[32,1024]{1,0:T(8,128)(2,1)} all-gather(bf16[32,512]{1,0:T(8,128)(2,1)} %param.13), channel_id=1, replica_groups=mesh['seq'=16,'dp'=2] {'dp'}, dimensions={1}, use_global_device_ids=true | all-gather | bytes 98304 | tf_op jit(solution)/shard_map/all_gather | solution.py:54
  12.9 1.8 fusion.1
  15.6 4.5 %collective-permute-start = (bf16[1,15,512]{2,1,0:T(8,128)(2,1)S(1)}, bf16[1,15,512]{2,1,0:T(8,128)(2,1)S(1)}, u32[]{:S(2)}, u32[]{:S(2)}) collective-permute-start(bf16[1,15,512]{2,1,0:T(8,128)(2,1)S(1)} %get-tuple-element.60), channel_id=1, source_target_pairs={{0,2},{2,4},{4,6},{6,8},{8,10},{10,12},{12,14},{14,16},{16,18},{18... | collective-permute-start | bytes 46088 | tf_op jit(solution)/shard_map/ppermute | solution.py:14
  20.2 1.3 collective-permute-start.1
  22.9 3.0 %collective-permute-done.1 = bf16[1,15,512]{2,1,0:T(8,128)(2,1)S(1)} collective-permute-done((bf16[1,15,512]{2,1,0:T(8,128)(2,1)S(1)}, bf16[1,15,512]{2,1,0:T(8,128)(2,1)S(1)}, u32[]{:S(2)}, u32[]{:S(2)}) %collective-permute-start.1) | collective-permute-done | bytes 15392 | tf_op jit(solution)/shard_map/ppermute | solution.py:17
  25.9 1.4 maximum_convert_fusion
  27.3 7.4 %fusion.5 = (f32[512]{0:T(512)S(1)}, f32[512]{0:T(512)S(1)}, f32[1,768,512]{2,1,0:T(8,128)}) fusion(f32[768]{0:T(1024)S(1)} %fusion.80, f32[1,798,512]{2,1,0:T(8,128)S(1)} %maximum_convert_fusion, f32[512]{0:T(512)S(1)} %bitcast.139, f32[512]{0:T(512)S(1)} %bitcast.141, f32[512]{0:T(512)S(1)} %bitcast.83, f32[512]{0:T(512)S(1)} %bitcast.85, ...), kind=kLoop, calls=%fused_computation.41 | loop fusion | flops 25558016 | bytes 50402304 | tf_op jit(solution)/shard_map/reduce_sum | solution.py:43
  34.7 42.6 %all-reduce.1 = (f32[512]{0:T(512)S(1)}, f32[512]{0:T(512)S(1)}) all-reduce(f32[512]{0:T(512)S(1)} %get-tuple-element.47, f32[512]{0:T(512)S(1)} %get-tuple-element.46), channel_id=1, replica_groups=mesh['seq'=16,'dp'=2] {'seq','dp'}, use_global_device_ids=true, to_apply=%region_4.0 | all-reduce | flops 1024 | bytes 8192 | tf_op jit(solution)/shard_map/psum | solution.py:40
  77.3 3.9 %convolution_multiply_fusion = f32[512,1024]{1,0:T(8,128)} fusion(bf16[1,768,1024]{2,1,0:T(8,128)(2,1)S(1)} %copy-done, f32[1,768,512]{2,1,0:T(8,128)} %get-tuple-element.57, f32[512]{0:T(512)S(1)} %copy-done.9, f32[512]{0:T(512)S(1)} %get-tuple-element.94, f32[512]{0:T(512)S(1)} %copy-done.8, f32[512]{0:T(512)S(1)} %get-tuple-element.93, f32[768]{0:T(1024)S(1)} %fusion.80), kind=kOutput, calls=%fused_computation.35 | convolution fusion | flops 809762816 | bytes 5254144 | tf_op jit(solution)/shard_map/btc,btd->cd/dot_general | solution.py:73
  81.3 4.5 %fusion.82 = (f32[512]{0:T(512)S(1)}, f32[512]{0:T(512)S(1)}, f32[1,768,512]{2,1,0:T(8,128)}) fusion(f32[512]{0:T(512)S(1)} %get-tuple-element.93, f32[1,768,512]{2,1,0:T(8,128)} %get-tuple-element.57, f32[512]{0:T(512)S(1)} %get-tuple-element.94, f32[512]{0:T(512)S(1)} %copy-done.9, f32[512]{0:T(512)S(1)} %copy-done.8, ...), kind=kOutput, calls=%fused_computation.168 | convolution fusion | flops 811596800 | bytes 5782528 | tf_op jit(solution)/shard_map/btd,cd->btc/dot_general | solution.py:55
  85.8 40.4 %all-reduce = (f32[512]{0:T(512)S(1)}, f32[512]{0:T(512)S(1)}) all-reduce(f32[512]{0:T(512)S(1)} %get-tuple-element.49, f32[512]{0:T(512)S(1)} %get-tuple-element.48), channel_id=1, replica_groups=mesh['seq'=16,'dp'=2] {'seq','dp'}, use_global_device_ids=true, to_apply=%region_8.0 | all-reduce | flops 1024 | bytes 8192 | tf_op jit(solution)/shard_map/psum | solution.py:62
  126.3 5.7 %fusion.36 = (f32[512]{0:T(512)S(1)}, f32[512]{0:T(512)S(1)}, f32[512]{0:T(512)S(1)}, f32[512]{0:T(512)S(1)}, f32[512]{0:T(512)S(1)}, /*index=5*/f32[512]{0:T(51...) fusion(f32[1,798,512]{2,1,0:T(8,128)S(1)} %maximum_convert_fusi, ...), kind=kLoop, calls=%fused_computation.72 | loop fusion | flops 18471936 | bytes 32293892 | tf_op jit(solution)/shard_map/reduce_sum | solution.py:79
  132.1 4.2 %collective-permute-start.2 = (bf16[1,15,512]{2,1,0:T(8,128)(2,1)S(1)}, bf16[1,15,512]{2,1,0:T(8,128)(2,1)S(1)}, u32[]{:S(2)}, u32[]{:S(2)}) collective-permute-start(bf16[1,15,512]{2,1,0:T(8,128)(2,1)S(1)} %get-tuple-element.58), channel_id=1, source_target_pairs={{0,2},{2,4},{4,6},{6,8},{8,10},{10,12},{12,14},{14,16},{16,18},{18... | collective-permute-start | bytes 46088 | tf_op jit(solution)/shard_map/ppermute | solution.py:14
  137.5 3.2 %fusion.35 = (f32[512]{0:T(512)S(1)}, f32[512]{0:T(512)S(1)}, f32[512]{0:T(512)}, f32[512]{0:T(512)}, f32[512]{0:T(512)}, /*index=5*/f32[512]{0:T(512)}, f32[512...) fusion(bf16[1,768,512]{2,1,0:T(8,128)(2,1)S(1)} %get-tuple-element.54, ...), kind=kLoop, calls=%fused_computation.71 | loop fusion | flops 10610176 | bytes 21260288 | tf_op jit(solution)/shard_map/reduce_sum | solution.py:79
  140.7 2.2 stack.127
  143.0 1.4 dynamic-slice_multiply_fusion
  145.5 1.4 maximum_convert_fusion.1
  146.9 7.6 %multiply_convert_fusion.1 = (bf16[1,768,512]{2,1,0:T(8,128)(2,1)}, f32[1,768,512]{2,1,0:T(8,128)}) fusion(bf16[1,768,1024]{2,1,0:T(8,128)(2,1)S(1)} %copy-done.1, f32[768]{0:T(1024)S(1)} %fusion.80, f32[1,798,512]{2,1,0:T(8,128)S(1)} %maximum_convert_fusion.1, f32[512]{0:T(512)S(1)} %bitcast.140, f32[512]{0:T(512)S(1)} %bitcast.142, f32[512]{0:T(512)S(1)} %bitcast.84, ...), kind=kLoop, calls=%fused_computation.142 | loop fusion | flops 26738688 | bytes 51971072 | tf_op jit(solution)/shard_map/convert
  154.5 7.9 %reduce-scatter.6.cloned.1.call-done = f32[32,1024]{1,0:T(8,128)} async-done(((f32[512,1024]{1,0:T(8,128)}), f32[32,1024]{1,0:T(8,128)}) %reduce-scatter.6.cloned.1.call-update) | async-done | bytes 131088 | tf_op jit(solution)/shard_map/reduce_scatter | solution.py:99
  162.5 2.0 fusion.4
  164.5 1.4 pad_maximum_fusion
  165.9 73.1 %reduce-scatter.10.cloned.1.call-done = f32[32,31]{1,0:T(8,128)} async-done(((f32[512,31]{1,0:T(8,128)}), f32[32,31]{1,0:T(8,128)}) %reduce-scatter.10.cloned.1.call-update) | async-done | bytes 3984
  239.7 3.4 %psum.39 = f32[32,31]{0,1:T(8,128)S(1)} all-reduce(f32[32,31]{0,1:T(8,128)S(1)} %copy.15), channel_id=1, replica_groups=mesh['seq'=16,'dp'=2] {'dp'}, use_global_device_ids=true, to_apply=%region_43.0 | all-reduce | flops 992 | bytes 7936 | tf_op jit(solution)/shard_map/psum | solution.py:103
  243.8 1.7 reduce-scatter.8.cloned.1.call-done
  (48 shorter events, 7.6 us)
Async XLA Ops:
  7.2 70.1 %copy-start = (bf16[1,768,1024]{2,1,0:T(8,128)(2,1)S(1)}, bf16[1,768,1024]{2,1,0:T(8,128)(2,1)}, u32[]{:S(2)}) copy-start(bf16[1,768,1024]{2,1,0:T(8,128)(2,1)} %param.8) | copy-start | bytes 4718596
  7.2 14.4 %copy-start.10 = (s32[2]{0:T(128)S(1)}, s32[2]{0:T(128)}, u32[]{:S(2)}) copy-start(s32[2]{0:T(128)} %param.9) | copy-start | bytes 28
  7.2 14.3 %copy-start.5 = (f32[512,31]{0,1:T(8,128)S(1)}, f32[512,31]{0,1:T(8,128)}, u32[]{:S(2)}) copy-start(f32[512,31]{0,1:T(8,128)} %param.10) | copy-start | bytes 190468
  7.2 74.1 %all-gather.2.cloned.1.call-start = ((), (), s32[]{:S(2)}) async-start(), calls=%async_computation.3 | async-start | bytes 1114112 | tf_op jit(solution)/shard_map/all_gather | solution.py:58
  11.0 151.5 %reduce-scatter.6.cloned.1.call-start = ((), (), s32[]{:S(2)}) async-start(), calls=%async_computation.4 | async-start | bytes 2228224 | tf_op jit(solution)/shard_map/reduce_scatter | solution.py:99
  14.7 0.9 copy-start.3
  15.6 7.2 %collective-permute-start = (bf16[1,15,512]{2,1,0:T(8,128)(2,1)S(1)}, bf16[1,15,512]{2,1,0:T(8,128)(2,1)S(1)}, u32[]{:S(2)}, u32[]{:S(2)}) collective-permute-start(bf16[1,15,512]{2,1,0:T(8,128)(2,1)S(1)} %get-tuple-element.60), channel_id=1, source_target_pairs={{0,2},{2,4},{4,6},{6,8},{8,10},{10,12},{12,14},{14,16},{16,18},{18... | collective-permute-start | bytes 46088 | tf_op jit(solution)/shard_map/ppermute | solution.py:14
  20.2 5.7 %collective-permute-start.1 = (bf16[1,15,512]{2,1,0:T(8,128)(2,1)S(1)}, bf16[1,15,512]{2,1,0:T(8,128)(2,1)S(1)}, u32[]{:S(2)}, u32[]{:S(2)}) collective-permute-start(bf16[1,15,512]{2,1,0:T(8,128)(2,1)S(1)} %get-tuple-element.61), channel_id=1, source_target_pairs={{2,0},{4,2},{6,4},{8,6},{10,8},{12,10},{14,12},{16,14},{18,16},{20... | collective-permute-start | bytes 46088 | tf_op jit(solution)/shard_map/ppermute | solution.py:17
  27.2 50.0 %copy-start.8 = (f32[512]{0:T(512)S(1)}, f32[512]{0:T(512)}, u32[]{:S(2)}) copy-start(f32[512]{0:T(512)} %param.11) | copy-start | bytes 6148
  27.2 50.0 %copy-start.9 = (f32[512]{0:T(512)S(1)}, f32[512]{0:T(512)}, u32[]{:S(2)}) copy-start(f32[512]{0:T(512)} %param.12) | copy-start | bytes 6148
  81.2 157.7 %reduce-scatter.10.cloned.1.call-start = ((), (), s32[]{:S(2)}) async-start(), calls=%async_computation.6 | async-start | bytes 278528
  126.3 5.7 %copy-start.6 = (f32[512]{0:T(512)}, f32[512]{0:T(512)S(1)}, u32[]{:S(2)}) copy-start(f32[512]{0:T(512)S(1)} %get-tuple-element.50) | copy-start | bytes 6148
  126.3 5.8 %copy-start.7 = (f32[512]{0:T(512)}, f32[512]{0:T(512)S(1)}, u32[]{:S(2)}) copy-start(f32[512]{0:T(512)S(1)} %get-tuple-element.51) | copy-start | bytes 6148
  132.0 8.7 %copy-start.2 = (bf16[1,768,512]{2,1,0:T(8,128)(2,1)}, bf16[1,768,512]{2,1,0:T(8,128)(2,1)S(1)}, u32[]{:S(2)}) copy-start(bf16[1,768,512]{2,1,0:T(8,128)(2,1)S(1)} %get-tuple-element.54) | copy-start | bytes 2359300
  132.1 13.4 %collective-permute-start.2 = (bf16[1,15,512]{2,1,0:T(8,128)(2,1)S(1)}, bf16[1,15,512]{2,1,0:T(8,128)(2,1)S(1)}, u32[]{:S(2)}, u32[]{:S(2)}) collective-permute-start(bf16[1,15,512]{2,1,0:T(8,128)(2,1)S(1)} %get-tuple-element.58), channel_id=1, source_target_pairs={{0,2},{2,4},{4,6},{6,8},{8,10},{10,12},{12,14},{14,16},{16,18},{18... | collective-permute-start | bytes 46088 | tf_op jit(solution)/shard_map/ppermute | solution.py:14
  136.2 9.3 %collective-permute-start.3 = (bf16[1,15,512]{2,1,0:T(8,128)(2,1)S(1)}, bf16[1,15,512]{2,1,0:T(8,128)(2,1)S(1)}, u32[]{:S(2)}, u32[]{:S(2)}) collective-permute-start(bf16[1,15,512]{2,1,0:T(8,128)(2,1)S(1)} %get-tuple-element.59), channel_id=1, source_target_pairs={{2,0},{4,2},{6,4},{8,6},{10,8},{12,10},{14,12},{16,14},{18,16},{20... | collective-permute-start | bytes 46088 | tf_op jit(solution)/shard_map/ppermute | solution.py:17
  143.0 3.9 %copy-start.1 = (bf16[1,768,1024]{2,1,0:T(8,128)(2,1)S(1)}, bf16[1,768,1024]{2,1,0:T(8,128)(2,1)}, u32[]{:S(2)}) copy-start(bf16[1,768,1024]{2,1,0:T(8,128)(2,1)} %param.7) | copy-start | bytes 4718596
  145.3 100.2 %reduce-scatter.8.cloned.1.call-start = ((), (), s32[]{:S(2)}) async-start(), calls=%async_computation.5 | async-start | bytes 196608 | tf_op jit(solution)/shard_map/reduce_scatter | solution.py:102
  162.4 2.0 copy-start.4
Sparse Core Ops, SparseCore 0:
  11.1 57.6 all-gather.1
  81.4 81.0 reduce-scatter.5
  164.7 74.2 reduce-scatter.9
  241.6 3.8 reduce-scatter.7
where the time goes:
time: 253 us; the launch traced here: 252 us
  blocking collectives  90.1 us (36%)
  waiting for transfers between devices  85.8 us (34%)
  other arithmetic  34.6 us (14%)
  between operations  14.7 us (6%)
  starting transfers between devices  11.6 us (5%)
  matrix products  8.43 us (3%)
  local copies, waits for them, and re-layouts  6.82 us (3%)
    unnamed x5, waiting for transfers between devices  73.1 us
    psum x1, blocking collectives, on_device(): lax.psum((jnp.sum(frame_mask * conv_out, axis=(0, 1)), jnp.sum(frame_mask...  42.6 us
    psum x1, blocking collectives, on_device(): lax.psum((jnp.sum(pre_grad * normed, axis=(0, 1)), jnp.sum(pre_grad, axis...  40.4 us
    another operation x2, other arithmetic  9.65 us
    reduce_sum x2, other arithmetic, on_device(): jnp.sum(conv_wide * padded[:, offset:offset + frames_dev], axis=(0, 1))  8.92 us
    ppermute x2, starting transfers between devices, with_halo(): lax.ppermute(lax.slice_in_dim(block, block.shape[dim] - width, None, axis...  8.69 us
    reduce_scatter x1, waiting for transfers between devices, on_device(): lax.psum_scatter(weight_terms, 'seq', scatter_dimension=0, tiled=True)  7.88 us
    reduce_sum x1, other arithmetic, on_device(): jnp.sum(frame_mask * conv_out * conv_out, axis=(0, 1))  7.41 us
  transfers between devices with their start and end apart: 8, of which 4 were waited for; matrix products, arithmetic and copies ran while one was open for 19% of the time, Pallas kernels for 0%

commit v1 on v0

v1 whole, which is shorter than its diff:
```python
import functools

import jax
import jax.numpy as jnp
from jax import lax
from jax.experimental import pallas as pl
from jax.experimental.pallas import tpu as pltpu
from jax.sharding import PartitionSpec as P

EPSILON = 1e-05
LANES = 128
EDGE = 16
MESH = pl.DeviceIdType.MESH


class Exchange:
    def __init__(self, axis, count, me, source, target, landed, send, recv):
        self.axis, self.count, self.me = axis, count, me
        self.source, self.target, self.landed = source, target, landed
        self.send, self.recv = send, recv

    def peer(self, step):
        return lax.rem(self.me + step, self.count)

    def start(self):
        def body(step, carry):
            peer = self.peer(step)
            pltpu.make_async_remote_copy(
                self.source(peer), self.target(), self.send.at[peer], self.recv.at[self.me],
                device_id={self.axis: peer}, device_id_type=MESH,
            ).start()
            return carry

        lax.fori_loop(1, self.count, body, 0)

    def wait(self, which):
        def body(step, carry):
            peer = self.peer(step)
            copy = pltpu.make_async_remote_copy(
                self.source(peer), self.landed(peer), self.send.at[peer], self.recv.at[peer],
                device_id={self.axis: peer}, device_id_type=MESH,
            )
            copy.wait_recv() if which == "recv" else copy.wait_send()
            return carry

        lax.fori_loop(1, self.count, body, 0)


def fused(dims, x_hbm, og_hbm, w_hbm, len_ref, taps_ref, gain_ref, shift_ref,
          in_out, proj_out, depth_out, sums_out,
          x, og, sig, pad, conv, act_grad, act, gpad, halo_s, halo_r, ghalo_s, ghalo_r,
          wall, w2, st1d, st1s, st2d, st2s, psend, prd, ps2, prs, dscr, dsend, drs, dd,
          in_sem, hs_sem, hr_sem, gs_sem, gr_sem, wgs, wgr, wds, wdr,
          a1, b1, a2, b2, a3, b3, a4, b4, pds, pdr, pss, psr, dss, dsr, dds, ddr):
    seq_n, dp_n, frames, channels, width, kernel, grad_scale = dims
    half = (kernel - 1) // 2
    blocks = channels // LANES
    rows, cols = channels // seq_n, width // dp_n
    seq, dp = lax.axis_index("seq"), lax.axis_index("dp")
    f32, bf16 = jnp.float32, jnp.bfloat16

    top = pltpu.make_async_copy(x_hbm.at[0, pl.ds(0, EDGE)], x.at[pl.ds(0, EDGE)], in_sem.at[0])
    bottom = pltpu.make_async_copy(
        x_hbm.at[0, pl.ds(frames - EDGE, EDGE)], x.at[pl.ds(frames - EDGE, EDGE)], in_sem.at[1]
    )
    middle = pltpu.make_async_copy(
        x_hbm.at[0, pl.ds(EDGE, frames - 2 * EDGE)],
        x.at[pl.ds(EDGE, frames - 2 * EDGE)], in_sem.at[2],
    )
    own_w = pltpu.make_async_copy(w_hbm, wall.at[dp, seq], in_sem.at[3])
    og_copy = pltpu.make_async_copy(og_hbm.at[0], og, in_sem.at[4])
    for copy in (top, bottom, own_w, middle, og_copy):
        copy.start()

    barrier = pltpu.get_barrier_semaphore()
    for axis, count, me in (("seq", seq_n, seq), ("dp", dp_n, dp)):
        def greet(step, carry):
            pl.semaphore_signal(barrier, inc=1, device_id={axis: lax.rem(me + step, count)},
                                device_id_type=MESH)
            return carry

        lax.fori_loop(1, count, greet, 0)

    length = len_ref[dp]
    total = lax.fori_loop(0, len_ref.shape[0], lambda i, s: s + len_ref[i], jnp.int32(0))
    inv_count = 1.0 / jnp.full((1, LANES), total.astype(f32), f32)
    first = seq * frames

    def mask_of(start, size):
        at = lax.broadcasted_iota(jnp.int32, (size, LANES), 0) + (first + start)
        return jnp.where(at < length, 1.0, 0.0).astype(f32)

    def glu(start, size, block):
        lanes = pl.ds(block * LANES, LANES)
        gates = pl.ds(channels + block * LANES, LANES)
        s = jax.nn.sigmoid(x[pl.ds(start, size), gates].astype(f32))
        sig[block, pl.ds(start, size), :] = s
        out = x[pl.ds(start, size), lanes].astype(f32) * s * mask_of(start, size)
        return out.astype(bf16)

    top.wait()
    bottom.wait()
    own_w.wait()
    for block in range(blocks):
        lanes = pl.ds(block * LANES, LANES)
        low, high = glu(0, EDGE, block), glu(frames - EDGE, EDGE, block)
        halo_s[0, :, lanes] = low
        halo_s[1, :, lanes] = high
        pad[block, pl.ds(EDGE, EDGE), :] = low.astype(f32)
        pad[block, pl.ds(frames, EDGE), :] = high.astype(f32)

    pl.semaphore_wait(barrier, seq_n + dp_n - 2)

    def halo_copy(which, send, recv, ssem, rsem):
        to = seq - 1 if which == 0 else seq + 1
        return pltpu.make_async_remote_copy(
            send.at[which], recv.at[1 - which], ssem.at[which], rsem.at[1 - which],
            device_id={"seq": to}, device_id_type=MESH,
        )

    def halo_start(*args):
        @pl.when(seq > 0)
        def _():
            halo_copy(0, *args).start()

        @pl.when(seq < seq_n - 1)
        def _():
            halo_copy(1, *args).start()

    def halo_wait(send, recv, ssem, rsem, into):
        @pl.when(seq > 0)
        def _():
            halo_copy(1, send, recv, ssem, rsem).wait_recv()
            for block in range(blocks):
                into[block, pl.ds(0, EDGE), :] = recv[0, :, pl.ds(block * LANES, LANES)].astype(f32)

        @pl.when(seq == 0)
        def _():
            for block in range(blocks):
                into[block, pl.ds(0, EDGE), :] = jnp.zeros((EDGE, LANES), f32)

        @pl.when(seq < seq_n - 1)
        def _():
            halo_copy(0, send, recv, ssem, rsem).wait_recv()
            for block in range(blocks):
                into[block, pl.ds(EDGE + frames, EDGE), :] = recv[
                    1, :, pl.ds(block * LANES, LANES)].astype(f32)

        @pl.when(seq == seq_n - 1)
        def _():
            for block in range(blocks):
                into[block, pl.ds(EDGE + frames, EDGE), :] = jnp.zeros((EDGE, LANES), f32)

    def halo_done(*args):
        @pl.when(seq > 0)
        def _():
            halo_copy(0, *args).wait_send()

        @pl.when(seq < seq_n - 1)
        def _():
            halo_copy(1, *args).wait_send()

    glu_halo = (halo_s, halo_r, hs_sem, hr_sem)
    grad_halo = (ghalo_s, ghalo_r, gs_sem, gr_sem)
    halo_start(*glu_halo)

    def exchange(axis, source, target, landed, send, recv):
        count, me = (seq_n, seq) if axis == "seq" else (dp_n, dp)
        return Exchange(axis, count, me, source, target, landed, send, recv)

    w_seq = exchange("seq", lambda p: wall.at[dp, seq], lambda: wall.at[dp, seq],
                     lambda p: wall.at[dp, p], wgs, wgr)
    w_dp = exchange("dp", lambda p: wall.at[dp], lambda: wall.at[dp], lambda p: wall.at[p],
                    wds, wdr)
    w_seq.start()

    middle.wait()
    chunk = 32
    inner = (frames - 2 * EDGE) // chunk

    def glu_body(i, carry):
        start = pl.multiple_of(EDGE + i * chunk, EDGE)
        for block in range(blocks):
            pad[block, pl.ds(EDGE + start, chunk), :] = glu(start, chunk, block).astype(f32)
        return carry

    lax.fori_loop(0, inner, glu_body, 0)
    halo_wait(*glu_halo, pad)

    def fold(v):
        return jnp.sum(v.reshape(v.shape[0] // 8, 8, LANES), axis=0)

    step_rows = 64
    steps = frames // step_rows

    def conv_block(block):
        lanes = pl.ds(block * LANES, LANES)

        def body(i, carry):
            start = pl.multiple_of(i * step_rows, step_rows)
            acc = jnp.zeros((step_rows, LANES), f32)
            for k in range(kernel):
                acc = acc + taps_ref[pl.ds(k, 1), lanes] * pad[
                    block, pl.ds(start + (EDGE - half + k), step_rows), :]
            conv[block, pl.ds(start, step_rows), :] = acc
            masked = acc * mask_of(start, step_rows)
            return carry[0] + fold(masked), carry[1] + fold(masked * acc)

        zero = jnp.zeros((8, LANES), f32)
        s, q = lax.fori_loop(0, steps, body, (zero, zero))
        return jnp.sum(s, axis=0, keepdims=True), jnp.sum(q, axis=0, keepdims=True)

    def reduce_pair(buf_d, buf_s, sems):
        d = exchange("dp", lambda p: buf_d.at[dp], lambda: buf_d.at[dp], lambda p: buf_d.at[p],
                     sems[0], sems[1])
        s = exchange("seq", lambda p: buf_s.at[seq], lambda: buf_s.at[seq], lambda p: buf_s.at[p],
                     sems[2], sems[3])
        return d, s

    def add_up(buf, count):
        return lax.fori_loop(1, count, lambda i, acc: acc + buf[i], buf[0])

    def stack(parts):
        first_half = jnp.concatenate([p[0] for p in parts], axis=0)
        return jnp.concatenate([first_half] + [p[1] for p in parts], axis=0)

    st1_dp, st1_seq = reduce_pair(st1d, st1s, (a1, b1, a2, b2))
    st1d[dp] = stack([conv_block(block) for block in range(blocks)])
    st1_dp.start()
    w_seq.wait("recv")
    w_dp.start()
    st1_dp.wait("recv")
    st1s[seq] = add_up(st1d, dp_n)
    st1_seq.start()

    w_dp.wait("recv")
    for d in range(dp_n):
        w2[:, pl.ds(d * cols, cols)] = wall[d].astype(f32).reshape(channels, cols).astype(bf16)
    og_copy.wait()
    mm_rows = 128

    def act_body(i, carry):
        at = pl.ds(pl.multiple_of(i * mm_rows, mm_rows), mm_rows)
        act_grad[at, :] = lax.dot_general(og[at, :], w2[...], (((1,), (1,)), ((), ())),
                                          preferred_element_type=f32)
        return carry

    lax.fori_loop(0, frames // mm_rows, act_body, 0)

    st1_seq.wait("recv")
    stats = add_up(st1s, seq_n)
    mean = stats[0:blocks] * inv_count
    variance = stats[blocks:] * inv_count - mean * mean
    inv_std = lax.rsqrt(variance + EPSILON)

    def pre_block(block):
        lanes = pl.ds(block * LANES, LANES)
        m, r = mean[block:block + 1], inv_std[block:block + 1]
        g, b = gain_ref[:, lanes], shift_ref[:, lanes]

        def body(i, carry):
            start = pl.multiple_of(i * step_rows, step_rows)
            at = pl.ds(start, step_rows)
            mask = mask_of(start, step_rows)
            normed = (conv[block, at, :] - m) * r
            pre_act = g * normed + b
            s = jax.nn.sigmoid(pre_act)
            act[at, lanes] = (mask * pre_act * s).astype(bf16)
            pre_grad = mask * act_grad[at, lanes] * s * (1.0 + pre_act * (1.0 - s))
            act_grad[at, lanes] = pre_grad
            return carry[0] + fold(pre_grad * normed), carry[1] + fold(pre_grad)

        zero = jnp.zeros((8, LANES), f32)
        s, q = lax.fori_loop(0, steps, body, (zero, zero))
        return jnp.sum(s, axis=0, keepdims=True), jnp.sum(q, axis=0, keepdims=True)

    st2_dp, st2_seq = reduce_pair(st2d, st2s, (a3, b3, a4, b4))
    st2d[dp] = stack([pre_block(block) for block in range(blocks)])
    st2_dp.start()

    per = LANES // rows
    p_dp = exchange("dp", lambda p: psend.at[p], lambda: prd.at[dp], lambda p: prd.at[p], pds, pdr)
    p_seq = exchange("seq", lambda p: ps2.at[p], lambda: prs.at[seq], lambda p: prs.at[p], pss, psr)

    def project(block):
        for d in range(dp_n):
            term = lax.dot_general(
                act[:, pl.ds(block * LANES, LANES)], og[:, pl.ds(d * cols, cols)],
                (((0,), (0,)), ((), ())), preferred_element_type=f32)
            psend[d, pl.ds(block * per, per)] = term.reshape(per, rows, cols).astype(bf16)

    for block in range(blocks // 2):
        project(block)
    st2_dp.wait("recv")
    st2s[seq] = add_up(st2d, dp_n)
    st2_seq.start()
    for block in range(blocks // 2, blocks):
        project(block)
    p_dp.start()

    st2_seq.wait("recv")
    sums = add_up(st2s, seq_n)
    sums_out[...] = sums * grad_scale
    gain_mean, shift_mean = sums[0:blocks] * inv_count, sums[blocks:] * inv_count

    def conv_grad(start, size, block):
        lanes = pl.ds(block * LANES, LANES)
        m, r = mean[block:block + 1], inv_std[block:block + 1]
        at = pl.ds(start, size)
        normed = (conv[block, at, :] - m) * r
        value = mask_of(start, size) * (r * gain_ref[:, lanes]) * (
            act_grad[at, lanes] - shift_mean[block:block + 1] - normed * gain_mean[block:block + 1])
        return value.astype(bf16)

    for block in range(blocks):
        lanes = pl.ds(block * LANES, LANES)
        low, high = conv_grad(0, EDGE, block), conv_grad(frames - EDGE, EDGE, block)
        ghalo_s[0, :, lanes] = low
        ghalo_s[1, :, lanes] = high
        gpad[block, pl.ds(EDGE, EDGE), :] = low.astype(f32)
        gpad[block, pl.ds(frames, EDGE), :] = high.astype(f32)
    halo_start(*grad_halo)

    def grad_body(i, carry):
        start = pl.multiple_of(EDGE + i * chunk, EDGE)
        for block in range(blocks):
            gpad[block, pl.ds(EDGE + start, chunk), :] = conv_grad(start, chunk, block).astype(f32)
        return carry

    lax.fori_loop(0, inner, grad_body, 0)

    p_dp.wait("recv")

    def add_dp(j, carry):
        def term(step, acc):
            return acc + prd[lax.rem(dp + step, dp_n), j].astype(f32)

        ps2[j] = lax.fori_loop(1, dp_n, term, psend[dp, j].astype(f32)).astype(bf16)
        return carry

    lax.fori_loop(0, seq_n, add_dp, 0)
    p_seq.start()

    small = 32
    d_seq = exchange("seq", lambda p: dsend.at[p], lambda: drs.at[seq], lambda p: drs.at[p],
                     dss, dsr)
    d_dp = exchange("dp", lambda p: dd.at[dp], lambda: dd.at[dp], lambda p: dd.at[p], dds, ddr)
    dscr[...] = jnp.zeros_like(dscr)
    for block in range(blocks):
        def depth_body(i, accs):
            start = pl.multiple_of(i * small, small)
            g = gpad[block, pl.ds(EDGE + start, small), :]
            return tuple(
                acc + fold(g * pad[block, pl.ds(start + (EDGE - half + k), small), :])
                for k, acc in enumerate(accs))

        accs = lax.fori_loop(0, frames // small, depth_body,
                             tuple(jnp.zeros((8, LANES), f32) for _ in range(kernel)))
        for k in range(kernel):
            dscr[pl.ds(k, 1), :] = jnp.sum(accs[k], axis=0, keepdims=True)
        dsend[pl.ds(block * per, per)] = jnp.transpose(dscr[...]).reshape(per, rows, LANES)
    d_seq.start()
    halo_wait(*grad_halo, gpad)

    def back_block(block):
        lanes = pl.ds(block * LANES, LANES)
        gates = pl.ds(channels + block * LANES, LANES)

        def body(i, carry):
            start = pl.multiple_of(i * step_rows, step_rows)
            at = pl.ds(start, step_rows)
            acc = jnp.zeros((step_rows, LANES), f32)
            for k in range(kernel):
                acc = acc + taps_ref[pl.ds(k, 1), lanes] * gpad[
                    block, pl.ds(start + (EDGE + half - k), step_rows), :]
            s = sig[block, at, :]
            scaled = acc * mask_of(start, step_rows) * s
            in_out[0, at, lanes] = scaled.astype(bf16)
            in_out[0, at, gates] = (scaled * x[at, lanes].astype(f32) * (1.0 - s)).astype(bf16)
            return carry

        lax.fori_loop(0, steps, body, 0)

    for block in range(blocks // 2):
        back_block(block)
    d_seq.wait("recv")
    dd[dp] = lax.fori_loop(
        1, seq_n, lambda i, acc: acc + drs[lax.rem(seq + i, seq_n)], dsend[seq])
    d_dp.start()
    for block in range(blocks // 2, blocks):
        back_block(block)

    p_seq.wait("recv")
    proj_out[...] = grad_scale * lax.fori_loop(
        1, seq_n, lambda i, acc: acc + prs[lax.rem(seq + i, seq_n)].astype(f32),
        ps2[seq].astype(f32))
    d_dp.wait("recv")
    depth_out[...] = grad_scale * add_up(dd, dp_n)

    halo_done(*glu_halo)
    halo_done(*grad_halo)
    for one in (w_seq, w_dp, st1_dp, st1_seq, st2_dp, st2_seq, p_dp, p_seq, d_seq, d_dp):
        one.wait("send")


def on_device(glu_input, out_grad, lengths, depth_weight, bn_gain, bn_shift, proj_weight):
    utts, frames, doubled = glu_input.shape
    channels, width = doubled // 2, out_grad.shape[2]
    kernel = depth_weight.shape[1]
    seq_n, dp_n = lax.axis_size("seq"), lax.axis_size("dp")
    rows, cols = channels // seq_n, width // dp_n
    blocks = channels // LANES
    assert utts == 1
    grad_scale = float(utts * dp_n * frames * seq_n) ** (-0.5)
    taps = jnp.transpose(depth_weight)
    f32, bf16 = jnp.float32, jnp.bfloat16
    vmem, dma = pltpu.VMEM, pltpu.SemaphoreType.DMA
    dims = (seq_n, dp_n, frames, channels, width, kernel, grad_scale)
    held = pl.BlockSpec(memory_space=pltpu.VMEM)
    apart = pl.BlockSpec(memory_space=pl.ANY)
    padded = frames + 2 * EDGE
    stat = (2 * blocks, LANES)
    input_grad, proj_grad, depth_grad, sums = pl.pallas_call(
        functools.partial(fused, dims),
        out_shape=(
            jax.ShapeDtypeStruct((1, frames, doubled), bf16),
            jax.ShapeDtypeStruct((rows, cols), f32),
            jax.ShapeDtypeStruct((rows, LANES), f32),
            jax.ShapeDtypeStruct(stat, f32),
        ),
        in_specs=[apart, apart, apart, pl.BlockSpec(memory_space=pltpu.SMEM), held, held, held],
        out_specs=(held, held, held, held),
        scratch_shapes=[
            vmem((frames, doubled), bf16),
            vmem((frames, width), bf16),
            vmem((blocks, frames, LANES), f32),
            vmem((blocks, padded, LANES), f32),
            vmem((blocks, frames, LANES), f32),
            vmem((frames, channels), f32),
            vmem((frames, channels), bf16),
            vmem((blocks, padded, LANES), f32),
            vmem((2, EDGE, channels), bf16),
            vmem((2, EDGE, channels), bf16),
            vmem((2, EDGE, channels), bf16),
            vmem((2, EDGE, channels), bf16),
            vmem((dp_n, seq_n, rows, cols), bf16),
            vmem((channels, width), bf16),
            vmem((dp_n,) + stat, f32),
            vmem((seq_n,) + stat, f32),
            vmem((dp_n,) + stat, f32),
            vmem((seq_n,) + stat, f32),
            vmem((dp_n, seq_n, rows, cols), bf16),
            vmem((dp_n, seq_n, rows, cols), bf16),
            vmem((seq_n, rows, cols), bf16),
            vmem((seq_n, rows, cols), bf16),
            vmem((LANES, LANES), f32),
            vmem((seq_n, rows, LANES), f32),
            vmem((seq_n, rows, LANES), f32),
            vmem((dp_n, rows, LANES), f32),
            dma((5,)), dma((2,)), dma((2,)), dma((2,)), dma((2,)),
            dma((seq_n,)), dma((seq_n,)), dma((dp_n,)), dma((dp_n,)),
            dma((dp_n,)), dma((dp_n,)), dma((seq_n,)), dma((seq_n,)),
            dma((dp_n,)), dma((dp_n,)), dma((seq_n,)), dma((seq_n,)),
            dma((dp_n,)), dma((dp_n,)), dma((seq_n,)), dma((seq_n,)),
            dma((seq_n,)), dma((seq_n,)), dma((dp_n,)), dma((dp_n,)),
        ],
        compiler_params=pltpu.CompilerParams(
            collective_id=0, has_side_effects=True, vmem_limit_bytes=56 * 1024 * 1024),
    )(glu_input, out_grad, proj_weight, lengths, taps, bn_gain[None], bn_shift[None])
    start = lax.axis_index("seq") * rows
    gain_grad = lax.dynamic_slice_in_dim(sums[:blocks].reshape(channels), start, rows)
    shift_grad = lax.dynamic_slice_in_dim(sums[blocks:].reshape(channels), start, rows)
    return input_grad, proj_grad, depth_grad[:, :kernel], gain_grad, shift_grad


def solution(mesh):
    return jax.shard_map(
        on_device,
        mesh=mesh,
        in_specs=(P("dp", "seq", None), P("dp", "seq", None), P(), P(), P(), P(), P("seq", "dp")),
        out_specs=(P("dp", "seq", None), P("seq", "dp"), P("seq", None), P("seq"), P("seq")),
        check_vma=False,
    )
```

time: 253 us -> 66.3 us (0.26)
  blocking collectives: 90.1 us -> 0 us
  waiting for transfers between devices: 85.8 us -> 0 us
  Pallas kernels: 0 us -> 59.5 us
  other arithmetic: 34.6 us -> 0 us
  between operations: 14.7 us -> 0.65 us
  starting transfers between devices: 11.6 us -> 0 us
  matrix products: 8.43 us -> 0 us
    psum x3 -> x0, blocking collectives: 86.4 us -> none  [the longest x1 42.6 us: on_device(): lax.psum((jnp.sum(frame_mask * conv_out, axis=(0, 1)), jnp.sum(frame_mask...]
    unnamed x5 -> x0, waiting for transfers between devices: 73.1 us -> none
    pallas_call x0 -> x1, Pallas kernels: none -> 59.5 us  [on_device(): pl.pallas_call(functools.partial(fused, dims), out_shape=(jax.ShapeDtypeS...]
    reduce_sum x4 -> x0, other arithmetic: 17 us -> none  [the longest x2 8.92 us: on_device(): jnp.sum(conv_wide * padded[:, offset:offset + frames_dev], axis=(0, 1))]
    ppermute x4 -> x0, starting transfers between devices: 11.3 us -> none  [the longest x2 8.69 us: with_halo(): lax.ppermute(lax.slice_in_dim(block, block.shape[dim] - width, None, axis...]
    another operation x2 -> x0, other arithmetic: 9.65 us -> none
    reduce_scatter x2 -> x0, waiting for transfers between devices: 9.6 us -> none  [the longest x1 7.88 us: on_device(): lax.psum_scatter(weight_terms, 'seq', scatter_dimension=0, tiled=True)]
    dot_general x2 -> x0, matrix products: 8.43 us -> none  [the longest x1 4.51 us: on_device(): jnp.einsum('btd,cd->btc', out_grad, lax.all_gather(proj_rows, 'seq', axis...]
  transfers between devices with their start and end apart: 8 -> 0, of which waited for: 4 -> 0; matrix products, arithmetic and copies ran while one was open for 19% -> 0% of each run, Pallas kernels for 0% -> 0%
where the time goes in v1:
time: 66.3 us; the launch traced here: 66 us
  Pallas kernels  59.5 us (90%)
  local copies, waits for them, and re-layouts  5.86 us (9%)
    pallas_call x1, Pallas kernels, on_device(): pl.pallas_call(functools.partial(fused, dims), out_shape=(jax.ShapeDtypeS...  59.5 us
    unnamed x7, local copies, waits for them, and re-layouts  3.94 us

profile of v1, /device:TPU:0, one launch (start us, length us, event | category | flops | bytes accessed | tf_op | source)
XLA Modules:
  0.0 66.0 jit_solution(6655121773674453623)
XLA Ops:
  0.6 59.5 %shard_map.110 = (bf16[1,768,1024]{2,1,0:T(8,128)(2,1)}, f32[32,512]{1,0:T(8,128)}, f32[32,128]{1,0:T(8,128)}, f32[8,128]{1,0:T(8,128)}) custom-call(bf16[1,768,1024]{2,1,0:T(8,128)(2,1)} %x_hbm.1, bf16[1,768,1024]{2,1,0:T(8,128)(2,1)} %og_hbm.1, bf16[32,512]{1,0:T(8,128)(2,1)} %w_hbm.1, s32[2]{0:T(128)} %len_ref.1, f32[31,512]{1,0:T(8,128)} %bitcast.8, ...), custom_call_target="tpu_custom_call" | custom-call | tf_op jit(solution)/shard_map/pallas_call | solution.py:423
  60.2 0.8 %slice_bitcast_fusion = (f32[512]{0:T(512)S(1)}, f32[512]{0:T(512)S(1)}) fusion(f32[8,128]{1,0:T(8,128)} %get-tuple-element.12), kind=kLoop, calls=%fused_computation | loop fusion | bytes 8192 | tf_op jit(solution)/shard_map/reshape | solution.py:472
  60.9 0.6 dynamic_slice.6
  61.5 0.6 dynamic_slice.7
  62.1 0.0 copy-start
  62.1 0.0 copy-start.1
  62.1 2.7 %copy.15 = bf16[1,768,1024]{2,1,0:T(8,128)(2,1)} copy(bf16[1,768,1024]{2,1,0:T(8,128)(2,1)} %get-tuple-element.20) | data formatting | bytes 3145728
  64.8 0.0 copy-done
  64.8 0.6 copy.16
  65.4 0.0 copy-done.1
  65.4 0.6 copy.17
Async XLA Ops:
  62.1 2.7 %copy-start = (f32[32,512]{1,0:T(8,128)S(1)}, f32[32,512]{1,0:T(8,128)}, u32[]{:S(2)}) copy-start(f32[32,512]{1,0:T(8,128)} %get-tuple-element.21) | copy-start | bytes 196612
  62.1 3.3 %copy-start.1 = (f32[32,128]{1,0:T(8,128)S(1)}, f32[32,128]{1,0:T(8,128)}, u32[]{:S(2)}) copy-start(f32[32,128]{1,0:T(8,128)} %get-tuple-element.11) | copy-start | bytes 49156

commit v2 on v1

--- a/solution.py
+++ b/solution.py
@@ -14,8 +14,8 @@
 
 
 class Exchange:
-    def __init__(self, axis, count, me, source, target, landed, send, recv):
-        self.axis, self.count, self.me = axis, count, me
+    def __init__(self, to, count, me, source, target, landed, send, recv):
+        self.to, self.count, self.me = to, count, me
         self.source, self.target, self.landed = source, target, landed
         self.send, self.recv = send, recv
 
@@ -27,7 +27,7 @@
             peer = self.peer(step)
             pltpu.make_async_remote_copy(
                 self.source(peer), self.target(), self.send.at[peer], self.recv.at[self.me],
-                device_id={self.axis: peer}, device_id_type=MESH,
+                device_id=self.to(peer), device_id_type=MESH,
             ).start()
             return carry
 
@@ -38,7 +38,7 @@
             peer = self.peer(step)
             copy = pltpu.make_async_remote_copy(
                 self.source(peer), self.landed(peer), self.send.at[peer], self.recv.at[peer],
-                device_id={self.axis: peer}, device_id_type=MESH,
+                device_id=self.to(peer), device_id_type=MESH,
             )
             copy.wait_recv() if which == "recv" else copy.wait_send()
             return carry
@@ -49,14 +49,17 @@
 def fused(dims, x_hbm, og_hbm, w_hbm, len_ref, taps_ref, gain_ref, shift_ref,
           in_out, proj_out, depth_out, sums_out,
           x, og, sig, pad, conv, act_grad, act, gpad, halo_s, halo_r, ghalo_s, ghalo_r,
-          wall, w2, st1d, st1s, st2d, st2s, psend, prd, ps2, prs, dscr, dsend, drs, dd,
-          in_sem, hs_sem, hr_sem, gs_sem, gr_sem, wgs, wgr, wds, wdr,
-          a1, b1, a2, b2, a3, b3, a4, b4, pds, pdr, pss, psr, dss, dsr, dds, ddr):
+          wall, w2, st1d, st1s, st2d, st2s, psend, prd, ps2, prl, ps3, prh, dscr, dturn, dd, dh, dhr, dl,
+          in_sem, hs_sem, hr_sem, gs_sem, gr_sem, whs, whr, wls, wlr, wds, wdr,
+          a1, b1, a2, b2, a3, b3, a4, b4, pds, pdr, pls, plr, phs, phr,
+          dds, ddr, dhs_sem, dhr_sem, dls_sem, dlr_sem):
     seq_n, dp_n, frames, channels, width, kernel, grad_scale = dims
     half = (kernel - 1) // 2
     blocks = channels // LANES
     rows, cols = channels // seq_n, width // dp_n
     seq, dp = lax.axis_index("seq"), lax.axis_index("dp")
+    high_n, low_n = blocks, seq_n // blocks
+    high, low = seq // low_n, lax.rem(seq, low_n)
     f32, bf16 = jnp.float32, jnp.bfloat16
 
     top = pltpu.make_async_copy(x_hbm.at[0, pl.ds(0, EDGE)], x.at[pl.ds(0, EDGE)], in_sem.at[0])
@@ -67,7 +70,7 @@
         x_hbm.at[0, pl.ds(EDGE, frames - 2 * EDGE)],
         x.at[pl.ds(EDGE, frames - 2 * EDGE)], in_sem.at[2],
     )
-    own_w = pltpu.make_async_copy(w_hbm, wall.at[dp, seq], in_sem.at[3])
+    own_w = pltpu.make_async_copy(w_hbm, wall.at[dp, high, low], in_sem.at[3])
     og_copy = pltpu.make_async_copy(og_hbm.at[0], og, in_sem.at[4])
     for copy in (top, bottom, own_w, middle, og_copy):
         copy.start()
@@ -103,11 +106,11 @@
     own_w.wait()
     for block in range(blocks):
         lanes = pl.ds(block * LANES, LANES)
-        low, high = glu(0, EDGE, block), glu(frames - EDGE, EDGE, block)
-        halo_s[0, :, lanes] = low
-        halo_s[1, :, lanes] = high
-        pad[block, pl.ds(EDGE, EDGE), :] = low.astype(f32)
-        pad[block, pl.ds(frames, EDGE), :] = high.astype(f32)
+        head, tail = glu(0, EDGE, block), glu(frames - EDGE, EDGE, block)
+        halo_s[0, :, lanes] = head
+        halo_s[1, :, lanes] = tail
+        pad[block, pl.ds(EDGE, EDGE), :] = head.astype(f32)
+        pad[block, pl.ds(frames, EDGE), :] = tail.astype(f32)
 
     pl.semaphore_wait(barrier, seq_n + dp_n - 2)
 
@@ -165,14 +168,21 @@
     halo_start(*glu_halo)
 
     def exchange(axis, source, target, landed, send, recv):
-        count, me = (seq_n, seq) if axis == "seq" else (dp_n, dp)
-        return Exchange(axis, count, me, source, target, landed, send, recv)
-
-    w_seq = exchange("seq", lambda p: wall.at[dp, seq], lambda: wall.at[dp, seq],
-                     lambda p: wall.at[dp, p], wgs, wgr)
+        count, me, to = {
+            "seq": (seq_n, seq, lambda p: {"seq": p}),
+            "dp": (dp_n, dp, lambda p: {"dp": p}),
+            "high": (high_n, high, lambda p: {"seq": p * low_n + low}),
+            "low": (low_n, low, lambda p: {"seq": high * low_n + p}),
+        }[axis]
+        return Exchange(to, count, me, source, target, landed, send, recv)
+
+    w_high = exchange("high", lambda p: wall.at[dp, high, low], lambda: wall.at[dp, high, low],
+                      lambda p: wall.at[dp, p, low], whs, whr)
+    w_low = exchange("low", lambda p: wall.at[dp, :, low], lambda: wall.at[dp, :, low],
+                     lambda p: wall.at[dp, :, p], wls, wlr)
     w_dp = exchange("dp", lambda p: wall.at[dp], lambda: wall.at[dp], lambda p: wall.at[p],
                     wds, wdr)
-    w_seq.start()
+    w_high.start()
 
     middle.wait()
     chunk = 32
@@ -185,6 +195,8 @@
         return carry
 
     lax.fori_loop(0, inner, glu_body, 0)
+    w_high.wait("recv")
+    w_low.start()
     halo_wait(*glu_halo, pad)
 
     def fold(v):
@@ -227,7 +239,7 @@
     st1_dp, st1_seq = reduce_pair(st1d, st1s, (a1, b1, a2, b2))
     st1d[dp] = stack([conv_block(block) for block in range(blocks)])
     st1_dp.start()
-    w_seq.wait("recv")
+    w_low.wait("recv")
     w_dp.start()
     st1_dp.wait("recv")
     st1s[seq] = add_up(st1d, dp_n)
@@ -278,16 +290,19 @@
     st2d[dp] = stack([pre_block(block) for block in range(blocks)])
     st2_dp.start()
 
-    per = LANES // rows
+    per = low_n
     p_dp = exchange("dp", lambda p: psend.at[p], lambda: prd.at[dp], lambda p: prd.at[p], pds, pdr)
-    p_seq = exchange("seq", lambda p: ps2.at[p], lambda: prs.at[seq], lambda p: prs.at[p], pss, psr)
+    p_low = exchange("low", lambda p: ps2.at[:, p], lambda: prl.at[low], lambda p: prl.at[p],
+                     pls, plr)
+    p_high = exchange("high", lambda p: ps3.at[p], lambda: prh.at[high], lambda p: prh.at[p],
+                      phs, phr)
 
     def project(block):
         for d in range(dp_n):
             term = lax.dot_general(
                 act[:, pl.ds(block * LANES, LANES)], og[:, pl.ds(d * cols, cols)],
                 (((0,), (0,)), ((), ())), preferred_element_type=f32)
-            psend[d, pl.ds(block * per, per)] = term.reshape(per, rows, cols).astype(bf16)
+            psend[d, block] = term.reshape(per, rows, cols).astype(bf16)
 
     for block in range(blocks // 2):
         project(block)
@@ -314,11 +329,11 @@
 
     for block in range(blocks):
         lanes = pl.ds(block * LANES, LANES)
-        low, high = conv_grad(0, EDGE, block), conv_grad(frames - EDGE, EDGE, block)
-        ghalo_s[0, :, lanes] = low
-        ghalo_s[1, :, lanes] = high
-        gpad[block, pl.ds(EDGE, EDGE), :] = low.astype(f32)
-        gpad[block, pl.ds(frames, EDGE), :] = high.astype(f32)
+        head, tail = conv_grad(0, EDGE, block), conv_grad(frames - EDGE, EDGE, block)
+        ghalo_s[0, :, lanes] = head
+        ghalo_s[1, :, lanes] = tail
+        gpad[block, pl.ds(EDGE, EDGE), :] = head.astype(f32)
+        gpad[block, pl.ds(frames, EDGE), :] = tail.astype(f32)
     halo_start(*grad_halo)
 
     def grad_body(i, carry):
@@ -331,21 +346,26 @@
 
     p_dp.wait("recv")
 
-    def add_dp(j, carry):
+    def add_dp(at, carry):
+        h, j = at // low_n, lax.rem(at, low_n)
+
         def term(step, acc):
-            return acc + prd[lax.rem(dp + step, dp_n), j].astype(f32)
-
-        ps2[j] = lax.fori_loop(1, dp_n, term, psend[dp, j].astype(f32)).astype(bf16)
+            return acc + prd[lax.rem(dp + step, dp_n), h, j].astype(f32)
+
+        ps2[h, j] = lax.fori_loop(1, dp_n, term, psend[dp, h, j].astype(f32)).astype(bf16)
         return carry
 
     lax.fori_loop(0, seq_n, add_dp, 0)
-    p_seq.start()
+    p_low.start()
 
     small = 32
-    d_seq = exchange("seq", lambda p: dsend.at[p], lambda: drs.at[seq], lambda p: drs.at[p],
-                     dss, dsr)
     d_dp = exchange("dp", lambda p: dd.at[dp], lambda: dd.at[dp], lambda p: dd.at[p], dds, ddr)
+    d_high = exchange("high", lambda p: dh.at[p], lambda: dhr.at[high], lambda p: dhr.at[p],
+                      dhs_sem, dhr_sem)
+    d_low = exchange("low", lambda p: dl.at[low], lambda: dl.at[low], lambda p: dl.at[p],
+                     dls_sem, dlr_sem)
     dscr[...] = jnp.zeros_like(dscr)
+    dd[dp] = jnp.zeros(dd.shape[1:], f32)
     for block in range(blocks):
         def depth_body(i, accs):
             start = pl.multiple_of(i * small, small)
@@ -357,9 +377,18 @@
         accs = lax.fori_loop(0, frames // small, depth_body,
                              tuple(jnp.zeros((8, LANES), f32) for _ in range(kernel)))
         for k in range(kernel):
-            dscr[pl.ds(k, 1), :] = jnp.sum(accs[k], axis=0, keepdims=True)
-        dsend[pl.ds(block * per, per)] = jnp.transpose(dscr[...]).reshape(per, rows, LANES)
-    d_seq.start()
+            dd[dp, block, pl.ds(k, 1), :] = jnp.sum(accs[k], axis=0, keepdims=True)
+    d_dp.start()
+    p_low.wait("recv")
+
+    def add_low(h, carry):
+        ps3[h] = lax.fori_loop(
+            1, low_n, lambda i, acc: acc + prl[lax.rem(low + i, low_n), h].astype(f32),
+            ps2[h, low].astype(f32)).astype(bf16)
+        return carry
+
+    lax.fori_loop(0, high_n, add_low, 0)
+    p_high.start()
     halo_wait(*grad_halo, gpad)
 
     def back_block(block):
@@ -381,25 +410,31 @@
 
         lax.fori_loop(0, steps, body, 0)
 
+    d_dp.wait("recv")
+    dh[...] = add_up(dd, dp_n)
+    d_high.start()
     for block in range(blocks // 2):
         back_block(block)
-    d_seq.wait("recv")
-    dd[dp] = lax.fori_loop(
-        1, seq_n, lambda i, acc: acc + drs[lax.rem(seq + i, seq_n)], dsend[seq])
-    d_dp.start()
+    d_high.wait("recv")
+    dl[low] = lax.fori_loop(
+        1, high_n, lambda i, acc: acc + dhr[lax.rem(high + i, high_n)], dh[high])
+    d_low.start()
     for block in range(blocks // 2, blocks):
         back_block(block)
 
-    p_seq.wait("recv")
+    p_high.wait("recv")
     proj_out[...] = grad_scale * lax.fori_loop(
-        1, seq_n, lambda i, acc: acc + prs[lax.rem(seq + i, seq_n)].astype(f32),
-        ps2[seq].astype(f32))
-    d_dp.wait("recv")
-    depth_out[...] = grad_scale * add_up(dd, dp_n)
+        1, high_n, lambda i, acc: acc + prh[lax.rem(high + i, high_n)].astype(f32),
+        ps3[high].astype(f32))
+    d_low.wait("recv")
+    dscr[pl.ds(0, dl.shape[1]), :] = add_up(dl, low_n)
+    dturn[...] = jnp.transpose(dscr[...])
+    depth_out[...] = grad_scale * dturn[pl.ds(pl.multiple_of(low * rows, rows), rows), :]
 
     halo_done(*glu_halo)
     halo_done(*grad_halo)
-    for one in (w_seq, w_dp, st1_dp, st1_seq, st2_dp, st2_seq, p_dp, p_seq, d_seq, d_dp):
+    for one in (w_high, w_low, w_dp, st1_dp, st1_seq, st2_dp, st2_seq, p_dp, p_low, p_high,
+                d_dp, d_high, d_low):
         one.wait("send")
 
 
@@ -410,7 +445,9 @@
     seq_n, dp_n = lax.axis_size("seq"), lax.axis_size("dp")
     rows, cols = channels // seq_n, width // dp_n
     blocks = channels // LANES
-    assert utts == 1
+    assert utts == 1 and seq_n % blocks == 0
+    high_n, low_n = blocks, seq_n // blocks
+    taps_up = -(-kernel // 8) * 8
     grad_scale = float(utts * dp_n * frames * seq_n) ** (-0.5)
     taps = jnp.transpose(depth_weight)
     f32, bf16 = jnp.float32, jnp.bfloat16
@@ -443,26 +480,30 @@
             vmem((2, EDGE, channels), bf16),
             vmem((2, EDGE, channels), bf16),
             vmem((2, EDGE, channels), bf16),
-            vmem((dp_n, seq_n, rows, cols), bf16),
+            vmem((dp_n, high_n, low_n, rows, cols), bf16),
             vmem((channels, width), bf16),
             vmem((dp_n,) + stat, f32),
             vmem((seq_n,) + stat, f32),
             vmem((dp_n,) + stat, f32),
             vmem((seq_n,) + stat, f32),
-            vmem((dp_n, seq_n, rows, cols), bf16),
-            vmem((dp_n, seq_n, rows, cols), bf16),
-            vmem((seq_n, rows, cols), bf16),
-            vmem((seq_n, rows, cols), bf16),
+            vmem((dp_n, high_n, low_n, rows, cols), bf16),
+            vmem((dp_n, high_n, low_n, rows, cols), bf16),
+            vmem((high_n, low_n, rows, cols), bf16),
+            vmem((low_n, high_n, rows, cols), bf16),
+            vmem((high_n, rows, cols), bf16),
+            vmem((high_n, rows, cols), bf16),
             vmem((LANES, LANES), f32),
-            vmem((seq_n, rows, LANES), f32),
-            vmem((seq_n, rows, LANES), f32),
-            vmem((dp_n, rows, LANES), f32),
+            vmem((LANES, LANES), f32),
+            vmem((dp_n, blocks, taps_up, LANES), f32),
+            vmem((blocks, taps_up, LANES), f32),
+            vmem((high_n, taps_up, LANES), f32),
+            vmem((low_n, taps_up, LANES), f32),
             dma((5,)), dma((2,)), dma((2,)), dma((2,)), dma((2,)),
-            dma((seq_n,)), dma((seq_n,)), dma((dp_n,)), dma((dp_n,)),
+            dma((high_n,)), dma((high_n,)), dma((low_n,)), dma((low_n,)), dma((dp_n,)), dma((dp_n,)),
             dma((dp_n,)), dma((dp_n,)), dma((seq_n,)), dma((seq_n,)),
             dma((dp_n,)), dma((dp_n,)), dma((seq_n,)), dma((seq_n,)),
-            dma((dp_n,)), dma((dp_n,)), dma((seq_n,)), dma((seq_n,)),
-            dma((seq_n,)), dma((seq_n,)), dma((dp_n,)), dma((dp_n,)),
+            dma((dp_n,)), dma((dp_n,)), dma((low_n,)), dma((low_n,)), dma((high_n,)), dma((high_n,)),
+            dma((dp_n,)), dma((dp_n,)), dma((high_n,)), dma((high_n,)), dma((low_n,)), dma((low_n,)),
         ],
         compiler_params=pltpu.CompilerParams(
             collective_id=0, has_side_effects=True, vmem_limit_bytes=56 * 1024 * 1024),

time: 66.3 us -> 57.8 us (0.87)
  Pallas kernels: 59.5 us -> 51 us
    pallas_call x1, Pallas kernels: 59.5 us -> 51 us  [on_device(): pl.pallas_call(functools.partial(fused, dims), out_shape=(jax.ShapeDtypeS...]
where the time goes in v2:
time: 57.8 us; the launch traced here: 57.6 us
  Pallas kernels  51 us (88%)
  local copies, waits for them, and re-layouts  5.86 us (10%)
  between operations  0.65 us (1%)
    pallas_call x1, Pallas kernels, on_device(): pl.pallas_call(functools.partial(fused, dims), out_shape=(jax.ShapeDtypeS...  51 us
    unnamed x7, local copies, waits for them, and re-layouts  3.94 us

profile of v2, /device:TPU:0, one launch (start us, length us, event | category | flops | bytes accessed | tf_op | source)
XLA Modules:
  0.0 57.6 jit_solution(4334879776578534337)
XLA Ops:
  0.6 51.0 %shard_map.110 = (bf16[1,768,1024]{2,1,0:T(8,128)(2,1)}, f32[32,512]{1,0:T(8,128)}, f32[32,128]{1,0:T(8,128)}, f32[8,128]{1,0:T(8,128)}) custom-call(bf16[1,768,1024]{2,1,0:T(8,128)(2,1)} %x_hbm.1, bf16[1,768,1024]{2,1,0:T(8,128)(2,1)} %og_hbm.1, bf16[32,512]{1,0:T(8,128)(2,1)} %w_hbm.1, s32[2]{0:T(128)} %len_ref.1, f32[31,512]{1,0:T(8,128)} %bitcast.8, ...), custom_call_target="tpu_custom_call" | custom-call | tf_op jit(solution)/shard_map/pallas_call | solution.py:460
  51.7 0.8 %slice_bitcast_fusion = (f32[512]{0:T(512)S(1)}, f32[512]{0:T(512)S(1)}) fusion(f32[8,128]{1,0:T(8,128)} %get-tuple-element.12), kind=kLoop, calls=%fused_computation | loop fusion | bytes 8192 | tf_op jit(solution)/shard_map/reshape | solution.py:513
  52.4 0.6 %dynamic_slice.6 = f32[32]{0:T(128)} dynamic-slice(f32[512]{0:T(512)S(1)} %get-tuple-element.14, s32[]{:T(128)S(6)} %select_n.4), dynamic_slice_sizes={32} | dynamic-slice | bytes 260 | tf_op jit(solution)/shard_map/dynamic_slice | solution.py:512
  53.0 0.6 %dynamic_slice.7 = f32[32]{0:T(128)} dynamic-slice(f32[512]{0:T(512)S(1)} %get-tuple-element.13, s32[]{:T(128)S(6)} %select_n.4), dynamic_slice_sizes={32} | dynamic-slice | bytes 260 | tf_op jit(solution)/shard_map/dynamic_slice | solution.py:513
  53.6 0.0 copy-start
  53.6 0.0 copy-start.1
  53.6 2.7 %copy.15 = bf16[1,768,1024]{2,1,0:T(8,128)(2,1)} copy(bf16[1,768,1024]{2,1,0:T(8,128)(2,1)} %get-tuple-element.20) | data formatting | bytes 3145728
  56.3 0.0 copy-done
  56.3 0.6 %copy.16 = f32[32,512]{1,0:T(8,128)} copy(f32[32,512]{1,0:T(8,128)S(1)} %copy-done) | data formatting | bytes 131072
  57.0 0.0 copy-done.1
  57.0 0.6 %copy.17 = f32[32,31]{1,0:T(8,128)} copy(f32[32,31]{1,0:T(8,128)S(1)} %bitcast.9) | data formatting | bytes 7936
Async XLA Ops:
  53.6 2.7 %copy-start = (f32[32,512]{1,0:T(8,128)S(1)}, f32[32,512]{1,0:T(8,128)}, u32[]{:S(2)}) copy-start(f32[32,512]{1,0:T(8,128)} %get-tuple-element.21) | copy-start | bytes 196612
  53.6 3.3 %copy-start.1 = (f32[32,128]{1,0:T(8,128)S(1)}, f32[32,128]{1,0:T(8,128)}, u32[]{:S(2)}) copy-start(f32[32,128]{1,0:T(8,128)} %get-tuple-element.11) | copy-start | bytes 49156

commit v3 on v2

--- a/solution.py
+++ b/solution.py
@@ -47,9 +47,9 @@
 
 
 def fused(dims, x_hbm, og_hbm, w_hbm, len_ref, taps_ref, gain_ref, shift_ref,
-          in_out, proj_out, depth_out, sums_out,
+          in_out, proj_out, depth_out, gain_out, bias_out,
           x, og, sig, pad, conv, act_grad, act, gpad, halo_s, halo_r, ghalo_s, ghalo_r,
-          wall, w2, st1d, st1s, st2d, st2s, psend, prd, ps2, prl, ps3, prh, dscr, dturn, dd, dh, dhr, dl,
+          wall, w2, st1d, st1s, st2d, st2s, psend, prd, ps2, prl, ps3, prh, dscr, dturn, dd, dh, dhr, dl, sums_ref,
           in_sem, hs_sem, hr_sem, gs_sem, gr_sem, whs, whr, wls, wlr, wds, wdr,
           a1, b1, a2, b2, a3, b3, a4, b4, pds, pdr, pls, plr, phs, phr,
           dds, ddr, dhs_sem, dhr_sem, dls_sem, dlr_sem):
@@ -315,7 +315,15 @@
 
     st2_seq.wait("recv")
     sums = add_up(st2s, seq_n)
-    sums_out[...] = sums * grad_scale
+    sums_ref[...] = sums * grad_scale
+
+    def own(row):
+        turned = pltpu.roll(jnp.broadcast_to(sums_ref[pl.ds(row, 1), :], (8, LANES)),
+                            lax.rem(LANES - low * rows, LANES), 1)
+        return turned[0:1, 0:rows]
+
+    gain_out[...] = own(high)
+    bias_out[...] = own(blocks + high)
     gain_mean, shift_mean = sums[0:blocks] * inv_count, sums[blocks:] * inv_count
 
     def conv_grad(start, size, block):
@@ -429,13 +437,23 @@
     d_low.wait("recv")
     dscr[pl.ds(0, dl.shape[1]), :] = add_up(dl, low_n)
     dturn[...] = jnp.transpose(dscr[...])
-    depth_out[...] = grad_scale * dturn[pl.ds(pl.multiple_of(low * rows, rows), rows), :]
+    depth_out[...] = (grad_scale * dturn[pl.ds(pl.multiple_of(low * rows, rows), rows), :])[:, :kernel]
 
     halo_done(*glu_halo)
     halo_done(*grad_halo)
     for one in (w_high, w_low, w_dp, st1_dp, st1_seq, st2_dp, st2_seq, p_dp, p_low, p_high,
                 d_dp, d_high, d_low):
         one.wait("send")
+
+
+def put_out(*refs):
+    sem = refs[-1]
+    count = (len(refs) - 1) // 2
+    copies = [pltpu.make_async_copy(refs[i], refs[count + i], sem.at[i]) for i in range(count)]
+    for copy in copies:
+        copy.start()
+    for copy in copies:
+        copy.wait()
 
 
 def on_device(glu_input, out_grad, lengths, depth_weight, bn_gain, bn_shift, proj_weight):
@@ -457,16 +475,13 @@
     apart = pl.BlockSpec(memory_space=pl.ANY)
     padded = frames + 2 * EDGE
     stat = (2 * blocks, LANES)
-    input_grad, proj_grad, depth_grad, sums = pl.pallas_call(
+    shapes = (((1, frames, doubled), bf16), ((rows, cols), f32), ((rows, kernel), f32),
+              ((1, rows), f32), ((1, rows), f32))
+    results = pl.pallas_call(
         functools.partial(fused, dims),
-        out_shape=(
-            jax.ShapeDtypeStruct((1, frames, doubled), bf16),
-            jax.ShapeDtypeStruct((rows, cols), f32),
-            jax.ShapeDtypeStruct((rows, LANES), f32),
-            jax.ShapeDtypeStruct(stat, f32),
-        ),
+        out_shape=tuple(pltpu.VMEM(shape, dtype) for shape, dtype in shapes),
         in_specs=[apart, apart, apart, pl.BlockSpec(memory_space=pltpu.SMEM), held, held, held],
-        out_specs=(held, held, held, held),
+        out_specs=(held,) * len(shapes),
         scratch_shapes=[
             vmem((frames, doubled), bf16),
             vmem((frames, width), bf16),
@@ -498,6 +513,7 @@
             vmem((blocks, taps_up, LANES), f32),
             vmem((high_n, taps_up, LANES), f32),
             vmem((low_n, taps_up, LANES), f32),
+            vmem(stat, f32),
             dma((5,)), dma((2,)), dma((2,)), dma((2,)), dma((2,)),
             dma((high_n,)), dma((high_n,)), dma((low_n,)), dma((low_n,)), dma((dp_n,)), dma((dp_n,)),
             dma((dp_n,)), dma((dp_n,)), dma((seq_n,)), dma((seq_n,)),
@@ -508,10 +524,14 @@
         compiler_params=pltpu.CompilerParams(
             collective_id=0, has_side_effects=True, vmem_limit_bytes=56 * 1024 * 1024),
     )(glu_input, out_grad, proj_weight, lengths, taps, bn_gain[None], bn_shift[None])
-    start = lax.axis_index("seq") * rows
-    gain_grad = lax.dynamic_slice_in_dim(sums[:blocks].reshape(channels), start, rows)
-    shift_grad = lax.dynamic_slice_in_dim(sums[blocks:].reshape(channels), start, rows)
-    return input_grad, proj_grad, depth_grad[:, :kernel], gain_grad, shift_grad
+    input_grad, proj_grad, depth_grad, gain_grad, shift_grad = pl.pallas_call(
+        put_out,
+        out_shape=tuple(jax.ShapeDtypeStruct(shape, dtype) for shape, dtype in shapes),
+        in_specs=[held] * len(shapes),
+        out_specs=(apart,) * len(shapes),
+        scratch_shapes=[dma((len(shapes),))],
+    )(*(pltpu.with_memory_space_constraint(r, pltpu.VMEM) for r in results))
+    return input_grad, proj_grad, depth_grad, gain_grad[0], shift_grad[0]
 
 
 def solution(mesh):

time: 57.8 us -> 51.9 us (0.90)
  local copies, waits for them, and re-layouts: 5.86 us -> 0 us
    unnamed x7 -> x0, local copies, waits for them, and re-layouts: 3.94 us -> none
    dynamic_slice x2 -> x0, local copies, waits for them, and re-layouts: 1.16 us -> none  [the longest x1 0.58 us: on_device(): lax.dynamic_slice_in_dim(sums[:blocks].reshape(channels), start, rows)]
    reshape x1 -> x0, local copies, waits for them, and re-layouts: 0.75 us -> none  [on_device(): sums[blocks:].reshape(channels)]
    pallas_call x1 -> x2, Pallas kernels: 51 us -> 51.1 us  [the longest x1 49.9 us: on_device(): pl.pallas_call(functools.partial(fused, dims), out_shape=tuple((pltpu.VME...]
where the time goes in v3:
time: 51.9 us; the launch traced here: 51.7 us
  Pallas kernels  51.1 us (98%)
  between operations  0.64 us (1%)
    pallas_call x1, Pallas kernels, on_device(): pl.pallas_call(functools.partial(fused, dims), out_shape=tuple((pltpu.VME...  49.9 us
    pallas_call x1, Pallas kernels, on_device(): pl.pallas_call(put_out, out_shape=tuple((jax.ShapeDtypeStruct(shape, dtyp...  1.2 us

profile of v3, /device:TPU:0, one launch (start us, length us, event | category | flops | bytes accessed | tf_op | source)
XLA Modules:
  0.0 51.7 jit_solution(537010497600362550)
XLA Ops:
  0.6 49.9 %shard_map.110 = (bf16[1,768,1024]{2,1,0:T(8,128)(2,1)S(1)}, f32[32,512]{1,0:T(8,128)S(1)}, f32[32,31]{1,0:T(8,128)S(1)}, f32[1,32]{1,0:T(1,128)S(1)}, f32[1,32]{1,0:T(1,128)S(1)}) custom-call(bf16[1,768,1024]{2,1,0:T(8,128)(2,1)} %x_hbm.1, bf16[1,768,1024]{2,1,0:T(8,128)(2,1)} %og_hbm.1, bf16[32,512]{1,0:T(8,128)(2,1)} %w_hbm.1, s32[2]{0:T(128)} %len_ref.1, ...), custom_call_target="tpu_custom_call" | custom-call | tf_op jit(solution)/shard_map/pallas_call | solution.py:480
  50.5 1.2 %shard_map.111 = (bf16[1,768,1024]{2,1,0:T(8,128)(2,1)}, f32[32,512]{1,0:T(8,128)}, f32[32,31]{1,0:T(8,128)}, f32[1,32]{1,0:T(1,128)}, f32[1,32]{1,0:T(1,128)}) custom-call(bf16[1,768,1024]{2,1,0:T(8,128)(2,1)S(1)} %get-tuple-element.15.refs_0_, f32[32,512]{1,0:T(8,128)S(1)} %get-tuple-element.16.refs_1_, f32[32,31]{1,0:T(8,128)S(1)} %get-tuple-element.17.refs_2_, ...), custom_call_target="tpu_custom_call" | custom-call | tf_op jit(solution)/shard_map/pallas_call | solution.py:527

commit v4 on v3

--- a/solution.py
+++ b/solution.py
@@ -49,7 +49,7 @@
 def fused(dims, x_hbm, og_hbm, w_hbm, len_ref, taps_ref, gain_ref, shift_ref,
           in_out, proj_out, depth_out, gain_out, bias_out,
           x, og, sig, pad, conv, act_grad, act, gpad, halo_s, halo_r, ghalo_s, ghalo_r,
-          wall, w2, st1d, st1s, st2d, st2s, psend, prd, ps2, prl, ps3, prh, dscr, dturn, dd, dh, dhr, dl, sums_ref,
+          wall, w2, st1d, st1s, st2d, st2s, psend, prd, ps2, prl, ps3, prh, dscr, dturn, dd, dh, dhr, dl, sums_ref, lead, odd, trail, mixed,
           in_sem, hs_sem, hr_sem, gs_sem, gr_sem, whs, whr, wls, wlr, wds, wdr,
           a1, b1, a2, b2, a3, b3, a4, b4, pds, pdr, pls, plr, phs, phr,
           dds, ddr, dhs_sem, dhr_sem, dls_sem, dlr_sem):
@@ -101,72 +101,6 @@
         out = x[pl.ds(start, size), lanes].astype(f32) * s * mask_of(start, size)
         return out.astype(bf16)
 
-    top.wait()
-    bottom.wait()
-    own_w.wait()
-    for block in range(blocks):
-        lanes = pl.ds(block * LANES, LANES)
-        head, tail = glu(0, EDGE, block), glu(frames - EDGE, EDGE, block)
-        halo_s[0, :, lanes] = head
-        halo_s[1, :, lanes] = tail
-        pad[block, pl.ds(EDGE, EDGE), :] = head.astype(f32)
-        pad[block, pl.ds(frames, EDGE), :] = tail.astype(f32)
-
-    pl.semaphore_wait(barrier, seq_n + dp_n - 2)
-
-    def halo_copy(which, send, recv, ssem, rsem):
-        to = seq - 1 if which == 0 else seq + 1
-        return pltpu.make_async_remote_copy(
-            send.at[which], recv.at[1 - which], ssem.at[which], rsem.at[1 - which],
-            device_id={"seq": to}, device_id_type=MESH,
-        )
-
-    def halo_start(*args):
-        @pl.when(seq > 0)
-        def _():
-            halo_copy(0, *args).start()
-
-        @pl.when(seq < seq_n - 1)
-        def _():
-            halo_copy(1, *args).start()
-
-    def halo_wait(send, recv, ssem, rsem, into):
-        @pl.when(seq > 0)
-        def _():
-            halo_copy(1, send, recv, ssem, rsem).wait_recv()
-            for block in range(blocks):
-                into[block, pl.ds(0, EDGE), :] = recv[0, :, pl.ds(block * LANES, LANES)].astype(f32)
-
-        @pl.when(seq == 0)
-        def _():
-            for block in range(blocks):
-                into[block, pl.ds(0, EDGE), :] = jnp.zeros((EDGE, LANES), f32)
-
-        @pl.when(seq < seq_n - 1)
-        def _():
-            halo_copy(0, send, recv, ssem, rsem).wait_recv()
-            for block in range(blocks):
-                into[block, pl.ds(EDGE + frames, EDGE), :] = recv[
-                    1, :, pl.ds(block * LANES, LANES)].astype(f32)
-
-        @pl.when(seq == seq_n - 1)
-        def _():
-            for block in range(blocks):
-                into[block, pl.ds(EDGE + frames, EDGE), :] = jnp.zeros((EDGE, LANES), f32)
-
-    def halo_done(*args):
-        @pl.when(seq > 0)
-        def _():
-            halo_copy(0, *args).wait_send()
-
-        @pl.when(seq < seq_n - 1)
-        def _():
-            halo_copy(1, *args).wait_send()
-
-    glu_halo = (halo_s, halo_r, hs_sem, hr_sem)
-    grad_halo = (ghalo_s, ghalo_r, gs_sem, gr_sem)
-    halo_start(*glu_halo)
-
     def exchange(axis, source, target, landed, send, recv):
         count, me, to = {
             "seq": (seq_n, seq, lambda p: {"seq": p}),
@@ -182,7 +116,73 @@
                      lambda p: wall.at[dp, :, p], wls, wlr)
     w_dp = exchange("dp", lambda p: wall.at[dp], lambda: wall.at[dp], lambda p: wall.at[p],
                     wds, wdr)
+
+    own_w.wait()
+    pl.semaphore_wait(barrier, seq_n + dp_n - 2)
+
     w_high.start()
+    top.wait()
+    bottom.wait()
+    for block in range(blocks):
+        lanes = pl.ds(block * LANES, LANES)
+        head, tail = glu(0, EDGE, block), glu(frames - EDGE, EDGE, block)
+        halo_s[0, :, lanes] = head
+        halo_s[1, :, lanes] = tail
+        pad[block, pl.ds(EDGE, EDGE), :] = head.astype(f32)
+        pad[block, pl.ds(frames, EDGE), :] = tail.astype(f32)
+
+    def halo_copy(which, send, recv, ssem, rsem):
+        to = seq - 1 if which == 0 else seq + 1
+        return pltpu.make_async_remote_copy(
+            send.at[which], recv.at[1 - which], ssem.at[which], rsem.at[1 - which],
+            device_id={"seq": to}, device_id_type=MESH,
+        )
+
+    def halo_start(*args):
+        @pl.when(seq > 0)
+        def _():
+            halo_copy(0, *args).start()
+
+        @pl.when(seq < seq_n - 1)
+        def _():
+            halo_copy(1, *args).start()
+
+    def halo_wait(send, recv, ssem, rsem, into):
+        @pl.when(seq > 0)
+        def _():
+            halo_copy(1, send, recv, ssem, rsem).wait_recv()
+            for block in range(blocks):
+                into[block, pl.ds(0, EDGE), :] = recv[0, :, pl.ds(block * LANES, LANES)].astype(f32)
+
+        @pl.when(seq == 0)
+        def _():
+            for block in range(blocks):
+                into[block, pl.ds(0, EDGE), :] = jnp.zeros((EDGE, LANES), f32)
+
+        @pl.when(seq < seq_n - 1)
+        def _():
+            halo_copy(0, send, recv, ssem, rsem).wait_recv()
+            for block in range(blocks):
+                into[block, pl.ds(EDGE + frames, EDGE), :] = recv[
+                    1, :, pl.ds(block * LANES, LANES)].astype(f32)
+
+        @pl.when(seq == seq_n - 1)
+        def _():
+            for block in range(blocks):
+                into[block, pl.ds(EDGE + frames, EDGE), :] = jnp.zeros((EDGE, LANES), f32)
+
+    def halo_done(*args):
+        @pl.when(seq > 0)
+        def _():
+            halo_copy(0, *args).wait_send()
+
+        @pl.when(seq < seq_n - 1)
+        def _():
+            halo_copy(1, *args).wait_send()
+
+    glu_halo = (halo_s, halo_r, hs_sem, hr_sem)
+    grad_halo = (ghalo_s, ghalo_r, gs_sem, gr_sem)
+    halo_start(*glu_halo)
 
     middle.wait()
     chunk = 32
@@ -194,9 +194,10 @@
             pad[block, pl.ds(EDGE + start, chunk), :] = glu(start, chunk, block).astype(f32)
         return carry
 
-    lax.fori_loop(0, inner, glu_body, 0)
+    lax.fori_loop(0, inner // 2, glu_body, 0)
     w_high.wait("recv")
     w_low.start()
+    lax.fori_loop(inner // 2, inner, glu_body, 0)
     halo_wait(*glu_halo, pad)
 
     def fold(v):
@@ -204,19 +205,68 @@
 
     step_rows = 64
     steps = frames // step_rows
+    pairs = step_rows // 2
+    split_rows = (frames + 2 * EDGE) // 2 // 10
+    assert EDGE == half + 1 and kernel % 2 == 1
+
+    def split(src):
+        def body(i, carry):
+            for block in range(blocks):
+                start = i * (2 * split_rows)
+                e = src[block, pl.ds(start, split_rows, stride=2), :]
+                o = src[block, pl.ds(start + 1, split_rows, stride=2), :]
+                later = src[block, pl.ds(start + 2, split_rows, stride=2), :]
+                at = pl.ds(pl.multiple_of(i * split_rows, 8), split_rows)
+                lead[block, at, :] = e - o
+                odd[block, at, :] = o
+                trail[block, at, :] = later - o
+            return carry
+
+        lax.fori_loop(0, 10, body, 0)
+
+    def mix(tap):
+        mixed[pl.ds(0, 1), :] = taps_ref[pl.ds(tap(1), 1), :]
+        for n in range(1, (kernel + 1) // 2):
+            mixed[pl.ds(n, 1), :] = (
+                taps_ref[pl.ds(tap(2 * n), 1), :] + taps_ref[pl.ds(tap(2 * n + 1), 1), :])
+
+    def filtered(block, i, tap):
+        lanes = pl.ds(block * LANES, LANES)
+        start = pl.multiple_of(i * pairs, pairs)
+        zero = jnp.zeros((pairs, LANES), f32)
+        one, two, three = zero, zero, zero
+        for n in range((kernel + 1) // 2):
+            at = pl.ds(start + n, pairs)
+            if n:
+                one = one + taps_ref[pl.ds(tap(2 * n), 1), lanes] * lead[block, at, :]
+            two = two + mixed[pl.ds(n, 1), lanes] * odd[block, at, :]
+            three = three + taps_ref[pl.ds(tap(2 * n + 1), 1), lanes] * trail[block, at, :]
+        first_row = i * step_rows
+        even, later = one + two, two + three
+        conv[block, pl.ds(first_row, pairs, stride=2), :] = even
+        conv[block, pl.ds(first_row + 1, pairs, stride=2), :] = later
+        return even, later
+
+    def forward(j):
+        return j - 1
+
+    def backward(j):
+        return kernel - j
+
+    mix(forward)
+    split(pad)
 
     def conv_block(block):
         lanes = pl.ds(block * LANES, LANES)
 
         def body(i, carry):
-            start = pl.multiple_of(i * step_rows, step_rows)
-            acc = jnp.zeros((step_rows, LANES), f32)
-            for k in range(kernel):
-                acc = acc + taps_ref[pl.ds(k, 1), lanes] * pad[
-                    block, pl.ds(start + (EDGE - half + k), step_rows), :]
-            conv[block, pl.ds(start, step_rows), :] = acc
-            masked = acc * mask_of(start, step_rows)
-            return carry[0] + fold(masked), carry[1] + fold(masked * acc)
+            even, later = filtered(block, i, forward)
+            at = 2 * lax.broadcasted_iota(jnp.int32, (pairs, LANES), 0) + (
+                first + i * step_rows)
+            m_even = jnp.where(at < length, even, 0.0)
+            m_later = jnp.where(at + 1 < length, later, 0.0)
+            return (carry[0] + fold(m_even + m_later),
+                    carry[1] + fold(m_even * m_even + m_later * m_later))
 
         zero = jnp.zeros((8, LANES), f32)
         s, q = lax.fori_loop(0, steps, body, (zero, zero))
@@ -313,6 +363,20 @@
         project(block)
     p_dp.start()
 
+    p_dp.wait("recv")
+
+    def add_dp(at, carry):
+        h, j = at // low_n, lax.rem(at, low_n)
+
+        def term(step, acc):
+            return acc + prd[lax.rem(dp + step, dp_n), h, j].astype(f32)
+
+        ps2[h, j] = lax.fori_loop(1, dp_n, term, psend[dp, h, j].astype(f32)).astype(bf16)
+        return carry
+
+    lax.fori_loop(0, seq_n, add_dp, 0)
+    p_low.start()
+
     st2_seq.wait("recv")
     sums = add_up(st2s, seq_n)
     sums_ref[...] = sums * grad_scale
@@ -351,20 +415,6 @@
         return carry
 
     lax.fori_loop(0, inner, grad_body, 0)
-
-    p_dp.wait("recv")
-
-    def add_dp(at, carry):
-        h, j = at // low_n, lax.rem(at, low_n)
-
-        def term(step, acc):
-            return acc + prd[lax.rem(dp + step, dp_n), h, j].astype(f32)
-
-        ps2[h, j] = lax.fori_loop(1, dp_n, term, psend[dp, h, j].astype(f32)).astype(bf16)
-        return carry
-
-    lax.fori_loop(0, seq_n, add_dp, 0)
-    p_low.start()
 
     small = 32
     d_dp = exchange("dp", lambda p: dd.at[dp], lambda: dd.at[dp], lambda p: dd.at[p], dds, ddr)
@@ -398,6 +448,8 @@
     lax.fori_loop(0, high_n, add_low, 0)
     p_high.start()
     halo_wait(*grad_halo, gpad)
+    mix(backward)
+    split(gpad)
 
     def back_block(block):
         lanes = pl.ds(block * LANES, LANES)
@@ -406,10 +458,8 @@
         def body(i, carry):
             start = pl.multiple_of(i * step_rows, step_rows)
             at = pl.ds(start, step_rows)
-            acc = jnp.zeros((step_rows, LANES), f32)
-            for k in range(kernel):
-                acc = acc + taps_ref[pl.ds(k, 1), lanes] * gpad[
-                    block, pl.ds(start + (EDGE + half - k), step_rows), :]
+            filtered(block, i, backward)
+            acc = conv[block, at, :]
             s = sig[block, at, :]
             scaled = acc * mask_of(start, step_rows) * s
             in_out[0, at, lanes] = scaled.astype(bf16)
@@ -486,11 +536,11 @@
             vmem((frames, doubled), bf16),
             vmem((frames, width), bf16),
             vmem((blocks, frames, LANES), f32),
-            vmem((blocks, padded, LANES), f32),
+            vmem((blocks, padded + 8, LANES), f32),
             vmem((blocks, frames, LANES), f32),
             vmem((frames, channels), f32),
             vmem((frames, channels), bf16),
-            vmem((blocks, padded, LANES), f32),
+            vmem((blocks, padded + 8, LANES), f32),
             vmem((2, EDGE, channels), bf16),
             vmem((2, EDGE, channels), bf16),
             vmem((2, EDGE, channels), bf16),
@@ -514,6 +564,10 @@
             vmem((high_n, taps_up, LANES), f32),
             vmem((low_n, taps_up, LANES), f32),
             vmem(stat, f32),
+            vmem((blocks, padded // 2, LANES), f32),
+            vmem((blocks, padded // 2, LANES), f32),
+            vmem((blocks, padded // 2, LANES), f32),
+            vmem(((kernel + 1) // 2, channels), f32),
             dma((5,)), dma((2,)), dma((2,)), dma((2,)), dma((2,)),
             dma((high_n,)), dma((high_n,)), dma((low_n,)), dma((low_n,)), dma((dp_n,)), dma((dp_n,)),
             dma((dp_n,)), dma((dp_n,)), dma((seq_n,)), dma((seq_n,)),

time: 51.9 us -> 49.5 us (0.954)
  Pallas kernels: 51.1 us -> 48.6 us
    pallas_call x1, Pallas kernels: 49.9 us -> 47.4 us  [on_device(): pl.pallas_call(functools.partial(fused, dims), out_shape=tuple((pltpu.VME...]
where the time goes in v4:
time: 49.5 us; the launch traced here: 49.3 us
  Pallas kernels  48.6 us (98%)
  between operations  0.64 us (1%)
    pallas_call x1, Pallas kernels, on_device(): pl.pallas_call(functools.partial(fused, dims), out_shape=tuple((pltpu.VME...  47.4 us
    pallas_call x1, Pallas kernels, on_device(): pl.pallas_call(put_out, out_shape=tuple((jax.ShapeDtypeStruct(shape, dtyp...  1.2 us

profile of v4, /device:TPU:0, one launch (start us, length us, event | category | flops | bytes accessed | tf_op | source)
XLA Modules:
  0.0 49.3 jit_solution(4481166343831139659)
XLA Ops:
  0.6 47.4 %shard_map.110 = (bf16[1,768,1024]{2,1,0:T(8,128)(2,1)S(1)}, f32[32,512]{1,0:T(8,128)S(1)}, f32[32,31]{1,0:T(8,128)S(1)}, f32[1,32]{1,0:T(1,128)S(1)}, f32[1,32]{1,0:T(1,128)S(1)}) custom-call(bf16[1,768,1024]{2,1,0:T(8,128)(2,1)} %x_hbm.1, bf16[1,768,1024]{2,1,0:T(8,128)(2,1)} %og_hbm.1, bf16[32,512]{1,0:T(8,128)(2,1)} %w_hbm.1, s32[2]{0:T(128)} %len_ref.1, ...), custom_call_target="tpu_custom_call" | custom-call | tf_op jit(solution)/shard_map/pallas_call | solution.py:530
  48.1 1.2 %shard_map.111 = (bf16[1,768,1024]{2,1,0:T(8,128)(2,1)}, f32[32,512]{1,0:T(8,128)}, f32[32,31]{1,0:T(8,128)}, f32[1,32]{1,0:T(1,128)}, f32[1,32]{1,0:T(1,128)}) custom-call(bf16[1,768,1024]{2,1,0:T(8,128)(2,1)S(1)} %get-tuple-element.15.refs_0_, f32[32,512]{1,0:T(8,128)S(1)} %get-tuple-element.16.refs_1_, f32[32,31]{1,0:T(8,128)S(1)} %get-tuple-element.17.refs_2_, ...), custom_call_target="tpu_custom_call" | custom-call | tf_op jit(solution)/shard_map/pallas_call | solution.py:581
